TPU v7x, 512 devices: a whole 4x4x16 slice. The times are simulated.
512 devices in a mesh: event: 8 (over y, core), tile: 64 (over x, z).
Axes of the slice: x: 4, y: 4, z: 16, core: 2. Of those that a mesh axis runs over, the one named last changes fastest.
Arguments:
- surface_start: float32 [8, 512, 8192], P('event', 'tile'), may hold values from -6 to 6
- east_start: float32 [8, 512, 8192], P('event', 'tile'), may hold values from -5 to 5
- north_start: float32 [8, 512, 8192], P('event', 'tile'), may hold values from -5 to 5
- still_depth: float32 [512, 8192], P('tile'), may hold values from 1 to 4
- roughness: float32 [512, 8192], P('tile'), may hold values from 0.5 to 2
- wet_masks: int32 [8, 2, 512, 8192], P('event', None, 'tile'), may hold values 0 or 1
- gauge_tiles: int32 [8, 16384, 1], P('event', 'tile'), may hold values from 0 to 63; in each aligned block of 256 rows (0 to 255, 256 to 511, ..., all dimensions but the last counted through in order) at most 8 rows name the same one
- gauge_cells: int32 [8, 16384], P('event', 'tile'), may hold values from 0 to 65535
- gauge_values: float32 [8, 16384], P('event', 'tile'), may hold values from -6 to 6
- survey_surface: float32 [8, 512, 8192], P('event', 'tile'), may hold values from -6 to 6
Outputs:
- roughness_grad: float32 [512, 8192], P('tile', 'event')
Inputs may be any that keep to these rules, and one draw needn't show every extreme that they name: `gauge_tiles`: of the gauges of one event listed on one strip, at most 8 lie in any one strip, and some strip receives exactly 8.
All inputs are finite; a program needn't handle non-finite values. No bound on the sum of `wet_masks` on one device may be relied on, other than what follows from the above.
Results may differ from a plain program's by a relative error of at most 0.0003.
Values sent between devices are 32-bit elements; how exact they have to be, the bound alone decides.
No kernel may reach another device: no remote copies, remote signals or barrier semaphores. Data moves between devices by JAX's collectives and lax.ppermute only.
A program may use at most 64 MiB of HBM per device.

v0:
```python
import jax
import jax.numpy as jnp
from jax import lax
from jax.sharding import PartitionSpec as P

STEPS = 2


def shifted(value, axis, steps):
    count = lax.axis_size(axis)
    initial, last = (max(0, -steps), min(count, count - steps))
    return lax.ppermute(value, axis, [(source, source + steps) for source in range(initial, last)])


def padded_2(cells, sides, width):
    for axis, dim in sides:
        count = lax.axis_size(axis)
        ends = count - 1
        head = lax.slice_in_dim(cells, 0, width, axis=dim)
        tail = lax.slice_in_dim(cells, cells.shape[dim] - width, cells.shape[dim], axis=dim)
        cells = jnp.concatenate(
            [
                lax.ppermute(tail, axis, [(i, (i + 1) % count) for i in range(ends)]),
                cells,
                lax.ppermute(head, axis, [((i + 1) % count, i) for i in range(ends)]),
            ],
            axis=dim,
        )
    return cells


def interior(field):
    return field[1:-1]


def across(field):
    padded = jnp.pad(field, ((0, 0), (1, 1)))
    return padded[:, 2:] - padded[:, :-2]


def along(field):
    return field[2:] - field[:-2]


def advance(surface, east, north, depth_rows, rough_rows, wetness):
    depth_inner = interior(depth_rows)
    depth_safe = jnp.where(depth_inner > 0, depth_inner, 1.0)
    east_inner = interior(east)
    north_inner = interior(north)
    speed = jnp.sqrt(east_inner * east_inner + north_inner * north_inner + 1.0)
    rough_inner = interior(rough_rows)
    friction = 1.0 + 2.0 * rough_inner * rough_inner * speed / depth_safe ** (4.0 / 3.0)
    wet_inner = interior(wetness)
    new_east = wet_inner * (east_inner - 0.2 * depth_inner * across(interior(surface))) / friction
    new_north = wet_inner * (north_inner - 0.2 * depth_inner * along(surface)) / friction
    new_surface = interior(interior(surface)) - 0.25 * interior(wet_inner) * (
        interior(across(new_east)) + along(new_north)
    )
    return (new_surface, interior(new_east), interior(new_north))


def fold_rims(stacked, width):
    upper = stacked[:, :width]
    lower = stacked[:, stacked.shape[1] - width :]
    inner = stacked[:, width : stacked.shape[1] - width]
    from_below = shifted(upper, "tile", -1)
    from_above = shifted(lower, "tile", 1)
    inner = inner.at[:, inner.shape[1] - width :].add(from_below)
    return inner.at[:, :width].add(from_above)


def per_device(
    surface_start,
    east_start,
    north_start,
    still_depth,
    roughness,
    wet_masks,
    gauge_tiles,
    gauge_cells,
    gauge_values,
    survey_surface,
):
    row_count, col_count = still_depth.shape
    wet_float = wet_masks[0].astype(jnp.float32)
    statics = jnp.stack((still_depth, roughness))
    stored = []
    width = 2
    static_pad = padded_2(statics, (("tile", 1),), 2)
    surface, east, north = (surface_start[0], east_start[0], north_start[0])
    for step_index in range(STEPS):
        padded = padded_2(
            jnp.stack((surface, east, north, wet_float[step_index])), (("tile", 1),), 2
        )
        record = (padded[0], padded[1], padded[2], static_pad[0], static_pad[1], padded[3])
        stored.append(record)
        surface, east, north = advance(*record)
    strip_tiles = gauge_tiles[0, :, 0]
    tile_count = lax.axis_size("tile")
    listed = strip_tiles.shape[0]
    capacity = max(2, 2 * listed // tile_count)
    onehot = (strip_tiles[:, None] == jnp.arange(tile_count, dtype=jnp.int32)[None, :]).astype(
        jnp.int32
    )
    before = jnp.cumsum(onehot, axis=0) - onehot
    rank = jnp.sum(onehot * before, axis=1)
    slot = strip_tiles * capacity + rank
    cell_count = row_count * col_count
    send_cells = (
        jnp.full((tile_count * capacity,), cell_count, jnp.int32).at[slot].set(gauge_cells[0])
    )
    send_values = jnp.zeros((tile_count * capacity,), jnp.float32).at[slot].set(gauge_values[0])
    got_cells, got_values = (
        lax.all_to_all(
            send_cells.reshape(tile_count, capacity),
            "tile",
            split_axis=0,
            concat_axis=0,
            tiled=True,
        ),
        lax.all_to_all(
            send_values.reshape(tile_count, capacity),
            "tile",
            split_axis=0,
            concat_axis=0,
            tiled=True,
        ),
    )
    flat_cells = got_cells.reshape(-1)
    valid = flat_cells < cell_count
    seen = jnp.take(surface.reshape(-1), flat_cells, mode="fill", fill_value=0.0)
    missing = jnp.where(valid, seen - got_values.reshape(-1), 0.0)
    gauge_sense = (
        jnp.zeros((cell_count,), jnp.float32)
        .at[flat_cells]
        .add(missing, mode="drop")
        .reshape(row_count, col_count)
    )
    sense_surface = gauge_sense + (surface - survey_surface[0])
    sense_east = jnp.zeros_like(sense_surface)
    sense_north = jnp.zeros_like(sense_surface)
    rough_sense = jnp.zeros((row_count + 2 * width, col_count), jnp.float32)
    for step_index in reversed(range(STEPS)):
        surface_in, east_in, north_in, depth_rows, rough_rows, wetness = stored[step_index]

        def local_step(surface_arg, east_arg, north_arg, rough_arg):
            return advance(surface_arg, east_arg, north_arg, depth_rows, rough_arg, wetness)

        outputs, pullback = jax.vjp(local_step, surface_in, east_in, north_in, rough_rows)
        back_surface, back_east, back_north, back_rough = pullback(
            (sense_surface, sense_east, sense_north)
        )
        rough_sense = rough_sense + back_rough
        if step_index > 0:
            folded = fold_rims(jnp.stack((back_surface, back_east, back_north)), 2)
            sense_surface, sense_east, sense_north = (folded[0], folded[1], folded[2])
    local_grad = fold_rims(rough_sense[None], width)[0]
    total = lax.psum(local_grad, "event")
    share = col_count // lax.axis_size("event")
    return lax.dynamic_slice_in_dim(total, lax.axis_index("event") * share, share, 1)


def solution(mesh):
    placed = (
        P("event", "tile", None),
        P("event", "tile", None),
        P("event", "tile", None),
        P("tile", None),
        P("tile", None),
        P("event", None, "tile", None),
        P("event", "tile", None),
        P("event", "tile"),
        P("event", "tile"),
        P("event", "tile", None),
    )
    return jax.shard_map(
        per_device, mesh=mesh, in_specs=placed, out_specs=P("tile", "event"), check_vma=False
    )
```

profile of v0, /device:TPU:2, one launch (start us, length us, event | category | flops | bytes accessed | tf_op | source)
XLA Modules:
  0.0 217.5 jit_solution(9492636156233918174)
XLA Ops:
  6.5 1.4 pad_maximum_fusion.31
  7.9 3.8 %collective-permute-start = (f32[2,2,8192]{2,1,0:T(2,128)S(1)}, f32[2,2,8192]{2,1,0:T(2,128)S(1)}, u32[]{:S(2)}, u32[]{:S(2)}) collective-permute-start(f32[2,2,8192]{2,1,0:T(2,128)S(1)} %get-tuple-element.102), channel_id=1, source_target_pairs={{0,1},{1,2},{2,3},{3,4},{4,5},{5,6},{6,7},{7,8},{8,9},{9,10},{10,1... | collective-permute-start | bytes 393224 | tf_op jit(solution)/shard_map/ppermute | solution.py:23
  11.7 9.5 %collective-permute-start.1 = (f32[2,2,8192]{2,1,0:T(2,128)S(1)}, f32[2,2,8192]{2,1,0:T(2,128)}, u32[]{:S(2)}, u32[]{:S(2)}) collective-permute-start(f32[2,2,8192]{2,1,0:T(2,128)S(1)} %get-tuple-element.103), channel_id=1, source_target_pairs={{1,0},{2,1},{3,2},{4,3},{5,4},{6,5},{7,6},{8,7},{9,8},{10,9},{11,1... | collective-permute-start | bytes 393224 | tf_op jit(solution)/shard_map/ppermute | solution.py:25
  24.2 1.6 scatter_custom_fusion
  26.5 12.4 %all-to-all-start = ((s32[64,1,8]{2,1,0:T(1,128)}), s32[64,1,8]{2,1,0:T(1,128)S(1)}, u32[]{:S(2)}, u32[]{:S(2)}) async-start(s32[64,1,8]{2,1,0:T(1,128)} %bitcast.12), calls=%async_computation | async-start | bytes 65536 | tf_op jit(solution)/shard_map/all_to_all | solution.py:114
  40.0 1.6 scatter_custom_fusion.1
  42.3 10.1 %all-to-all-done = s32[64,1,8]{2,1,0:T(1,128)S(1)} async-done(((s32[64,1,8]{2,1,0:T(1,128)}), s32[64,1,8]{2,1,0:T(1,128)S(1)}, u32[]{:S(2)}, u32[]{:S(2)}) %all-to-all-start) | async-done | bytes 2080 | tf_op jit(solution)/shard_map/all_to_all | solution.py:114
  52.4 5.5 %all-to-all-start.1 = ((f32[64,1,8]{2,1,0:T(1,128)}), f32[64,1,8]{2,1,0:T(1,128)S(1)}, u32[]{:S(2)}, u32[]{:S(2)}) async-start(f32[64,1,8]{2,1,0:T(1,128)} %bitcast.32), calls=%async_computation.1 | async-start | bytes 65536 | tf_op jit(solution)/shard_map/all_to_all | solution.py:121
  58.9 3.4 %collective-permute-start.2 = (f32[4,2,8192]{2,1,0:T(2,128)}, f32[4,2,8192]{2,1,0:T(2,128)S(1)}, u32[]{:S(2)}, u32[]{:S(2)}) collective-permute-start(f32[4,2,8192]{2,1,0:T(2,128)} %get-tuple-element.88), channel_id=1, source_target_pairs={{0,1},{1,2},{2,3},{3,4},{4,5},{5,6},{6,7},{7,8},{8,9},{9,10},{10,1... | collective-permute-start | bytes 786440 | tf_op jit(solution)/shard_map/ppermute | solution.py:23
  62.2 4.6 %collective-permute-start.3 = (f32[4,2,8192]{2,1,0:T(2,128)}, f32[4,2,8192]{2,1,0:T(2,128)S(1)}, u32[]{:S(2)}, u32[]{:S(2)}) collective-permute-start(f32[4,2,8192]{2,1,0:T(2,128)} %get-tuple-element.89), channel_id=1, source_target_pairs={{1,0},{2,1},{3,2},{4,3},{5,4},{6,5},{7,6},{8,7},{9,8},{10,9},{11,1... | collective-permute-start | bytes 786440 | tf_op jit(solution)/shard_map/ppermute | solution.py:25
  68.3 3.0 %all-to-all-done.1 = f32[64,1,8]{2,1,0:T(1,128)S(1)} async-done(((f32[64,1,8]{2,1,0:T(1,128)}), f32[64,1,8]{2,1,0:T(1,128)S(1)}, u32[]{:S(2)}, u32[]{:S(2)}) %all-to-all-start.1) | async-done | bytes 2080 | tf_op jit(solution)/shard_map/all_to_all | solution.py:121
  72.7 1.3 pad_maximum_fusion.3
  75.8 2.0 fusion.58
  77.9 1.4 pad_slice_fusion.3
  79.6 2.6 %collective-permute-start.4 = (f32[4,2,8192]{2,1,0:T(2,128)S(1)}, f32[4,2,8192]{2,1,0:T(2,128)S(1)}, u32[]{:S(2)}, u32[]{:S(2)}) collective-permute-start(f32[4,2,8192]{2,1,0:T(2,128)S(1)} %get-tuple-element.86), channel_id=1, source_target_pairs={{0,1},{1,2},{2,3},{3,4},{4,5},{5,6},{6,7},{7,8},{8,9},{9,10},{10,1... | collective-permute-start | bytes 786440 | tf_op jit(solution)/shard_map/ppermute | solution.py:23
  82.2 5.5 %collective-permute-start.5 = (f32[4,2,8192]{2,1,0:T(2,128)S(1)}, f32[4,2,8192]{2,1,0:T(2,128)S(1)}, u32[]{:S(2)}, u32[]{:S(2)}) collective-permute-start(f32[4,2,8192]{2,1,0:T(2,128)S(1)} %get-tuple-element.87), channel_id=1, source_target_pairs={{1,0},{2,1},{3,2},{4,3},{5,4},{6,5},{7,6},{8,7},{9,8},{10,9},{11,1... | collective-permute-start | bytes 786440 | tf_op jit(solution)/shard_map/ppermute | solution.py:25
  87.8 2.2 %collective-permute-done.4 = f32[4,2,8192]{2,1,0:T(2,128)S(1)} collective-permute-done((f32[4,2,8192]{2,1,0:T(2,128)S(1)}, f32[4,2,8192]{2,1,0:T(2,128)S(1)}, u32[]{:S(2)}, u32[]{:S(2)}) %collective-permute-start.4) | collective-permute-done | bytes 262176 | tf_op jit(solution)/shard_map/ppermute | solution.py:23
  90.0 1.5 collective-permute-done.5
  91.8 2.0 fusion.55
  97.1 3.1 %gather_fusion = f32[512]{0:T(512)S(1)} fusion(f32[65536]{0:T(1024)S(1)} %bitcast.247, s32[1024]{0:T(1024)S(1)} %pad_clamp_fusion), kind=kCustom, calls=%fused_computation | custom fusion | bytes 6144 | tf_op jit(solution)/shard_map/jit(_take)/gather | solution.py:131
  100.3 3.9 %scatter_custom_fusion.2 = f32[65536]{0:T(1024)} fusion(s32[512]{0:T(512)S(1)} %bitcast.260, f32[512]{0:T(512)S(1)} %subtract_select_fusion, f32[]{:T(128)} %constant.144.clone.1), kind=kCustom, calls=%fused_computation.127 | custom fusion | flops 512 | bytes 262148 | tf_op jit(solution)/shard_map/scatter-add | solution.py:136
  105.3 1.3 fusion.53
  106.8 1.7 fusion
  110.2 6.5 %collective-permute-start.6 = (f32[3,2,8192]{2,1,0:T(2,128)S(1)}, f32[3,2,8192]{2,1,0:T(2,128)S(1)}, u32[]{:S(2)}, u32[]{:S(2)}) collective-permute-start(f32[3,2,8192]{2,1,0:T(2,128)S(1)} %get-tuple-element.85), channel_id=1, source_target_pairs={{1,0},{2,1},{3,2},{4,3},{5,4},{6,5},{7,6},{8,7},{9,8},{10,9},{11,1... | collective-permute-start | bytes 589832 | tf_op jit(solution)/shard_map/ppermute | solution.py:12
  116.9 2.1 collective-permute-start.7
  120.1 6.6 %collective-permute-done.7 = f32[3,2,8192]{2,1,0:T(2,128)S(1)} collective-permute-done((f32[3,2,8192]{2,1,0:T(2,128)S(1)}, f32[3,2,8192]{2,1,0:T(2,128)S(1)}, u32[]{:S(2)}, u32[]{:S(2)}) %collective-permute-start.7) | collective-permute-done | bytes 196640 | tf_op jit(solution)/shard_map/ppermute | solution.py:12
  127.1 1.5 fusion.1
  128.9 1.9 collective-permute-start.8
  130.8 3.9 %collective-permute-start.9 = (f32[1,2,8192]{2,1,0:T(2,128)S(1)}, f32[1,2,8192]{2,1,0:T(2,128)S(1)}, u32[]{:S(2)}, u32[]{:S(2)}) collective-permute-start(f32[1,2,8192]{2,1,0:T(2,128)S(1)} %get-tuple-element.92), channel_id=1, source_target_pairs={{0,1},{1,2},{2,3},{3,4},{4,5},{5,6},{6,7},{7,8},{8,9},{9,10},{10,1... | collective-permute-start | bytes 196616 | tf_op jit(solution)/shard_map/ppermute | solution.py:12
  135.1 4.0 %collective-permute-done.9 = f32[1,2,8192]{2,1,0:T(2,128)S(1)} collective-permute-done((f32[1,2,8192]{2,1,0:T(2,128)S(1)}, f32[1,2,8192]{2,1,0:T(2,128)S(1)}, u32[]{:S(2)}, u32[]{:S(2)}) %collective-permute-start.9) | collective-permute-done | bytes 65568 | tf_op jit(solution)/shard_map/ppermute | solution.py:12
  139.9 69.4 %all-reduce.30.cloned.1.call-done = f32[8,8192]{1,0:T(8,128)} async-done(((f32[8,8192]{1,0:T(8,128)}), f32[8,8192]{1,0:T(8,128)}) %all-reduce.30.cloned.1.call-update) | async-done | bytes 262160 | tf_op jit(solution)/shard_map/psum | solution.py:158
  209.3 1.4 constant_dynamic-slice_fusion
  (111 shorter events, 20.9 us)
Async XLA Ops:
  6.5 51.3 %copy-start.9 = (f32[1,8,8192]{2,1,0:T(8,128)S(1)}, f32[1,8,8192]{2,1,0:T(8,128)}, u32[]{:S(2)}) copy-start(f32[1,8,8192]{2,1,0:T(8,128)} %param.18) | copy-start | bytes 786436
  6.5 51.3 %copy-start.12 = (f32[1,8,8192]{2,1,0:T(8,128)S(1)}, f32[1,8,8192]{2,1,0:T(8,128)}, u32[]{:S(2)}) copy-start(f32[1,8,8192]{2,1,0:T(8,128)} %param.19) | copy-start | bytes 786436
  6.5 51.4 %copy-start.10 = (f32[1,8,8192]{2,1,0:T(8,128)S(1)}, f32[1,8,8192]{2,1,0:T(8,128)}, u32[]{:S(2)}) copy-start(f32[1,8,8192]{2,1,0:T(8,128)} %param.20) | copy-start | bytes 786436
  7.9 64.8 %collective-permute-start = (f32[2,2,8192]{2,1,0:T(2,128)S(1)}, f32[2,2,8192]{2,1,0:T(2,128)S(1)}, u32[]{:S(2)}, u32[]{:S(2)}) collective-permute-start(f32[2,2,8192]{2,1,0:T(2,128)S(1)} %get-tuple-element.102), channel_id=1, source_target_pairs={{0,1},{1,2},{2,3},{3,4},{4,5},{5,6},{6,7},{7,8},{8,9},{9,10},{10,1... | collective-permute-start | bytes 393224 | tf_op jit(solution)/shard_map/ppermute | solution.py:23
  11.7 61.0 %collective-permute-start.1 = (f32[2,2,8192]{2,1,0:T(2,128)S(1)}, f32[2,2,8192]{2,1,0:T(2,128)}, u32[]{:S(2)}, u32[]{:S(2)}) collective-permute-start(f32[2,2,8192]{2,1,0:T(2,128)S(1)} %get-tuple-element.103), channel_id=1, source_target_pairs={{1,0},{2,1},{3,2},{4,3},{5,4},{6,5},{7,6},{8,7},{9,8},{10,9},{11,1... | collective-permute-start | bytes 393224 | tf_op jit(solution)/shard_map/ppermute | solution.py:25
  26.5 25.9 %all-to-all-start = ((s32[64,1,8]{2,1,0:T(1,128)}), s32[64,1,8]{2,1,0:T(1,128)S(1)}, u32[]{:S(2)}, u32[]{:S(2)}) async-start(s32[64,1,8]{2,1,0:T(1,128)} %bitcast.12), calls=%async_computation | async-start | bytes 65536 | tf_op jit(solution)/shard_map/all_to_all | solution.py:114
  40.0 39.3 %copy-start.2 = (f32[1,2,8,8192]{3,2,1,0:T(8,128)}, f32[1,2,8,8192]{3,2,1,0:T(8,128)S(1)}, u32[]{:S(2)}) copy-start(f32[1,2,8,8192]{3,2,1,0:T(8,128)S(1)} %convert_element_type.19) | copy-start | bytes 1572868
  52.4 19.0 %all-to-all-start.1 = ((f32[64,1,8]{2,1,0:T(1,128)}), f32[64,1,8]{2,1,0:T(1,128)S(1)}, u32[]{:S(2)}, u32[]{:S(2)}) async-start(f32[64,1,8]{2,1,0:T(1,128)} %bitcast.32), calls=%async_computation.1 | async-start | bytes 65536 | tf_op jit(solution)/shard_map/all_to_all | solution.py:121
  57.8 151.5 %all-reduce.30.cloned.1.call-start = ((), (), s32[]{:S(2)}) async-start(), calls=%async_computation.2 | async-start | bytes 524288 | tf_op jit(solution)/shard_map/psum | solution.py:158
  58.9 15.1 %collective-permute-start.2 = (f32[4,2,8192]{2,1,0:T(2,128)}, f32[4,2,8192]{2,1,0:T(2,128)S(1)}, u32[]{:S(2)}, u32[]{:S(2)}) collective-permute-start(f32[4,2,8192]{2,1,0:T(2,128)} %get-tuple-element.88), channel_id=1, source_target_pairs={{0,1},{1,2},{2,3},{3,4},{4,5},{5,6},{6,7},{7,8},{8,9},{9,10},{10,1... | collective-permute-start | bytes 786440 | tf_op jit(solution)/shard_map/ppermute | solution.py:23
  62.2 11.8 %collective-permute-start.3 = (f32[4,2,8192]{2,1,0:T(2,128)}, f32[4,2,8192]{2,1,0:T(2,128)S(1)}, u32[]{:S(2)}, u32[]{:S(2)}) collective-permute-start(f32[4,2,8192]{2,1,0:T(2,128)} %get-tuple-element.89), channel_id=1, source_target_pairs={{1,0},{2,1},{3,2},{4,3},{5,4},{6,5},{7,6},{8,7},{9,8},{10,9},{11,1... | collective-permute-start | bytes 786440 | tf_op jit(solution)/shard_map/ppermute | solution.py:25
  75.7 2.1 copy-start
  75.8 2.1 copy-start.11
  75.8 2.1 copy-start.13
  75.8 2.1 copy-start.19
  75.8 2.1 copy-start.21
  77.8 1.5 copy-start.7
  79.6 10.4 %collective-permute-start.4 = (f32[4,2,8192]{2,1,0:T(2,128)S(1)}, f32[4,2,8192]{2,1,0:T(2,128)S(1)}, u32[]{:S(2)}, u32[]{:S(2)}) collective-permute-start(f32[4,2,8192]{2,1,0:T(2,128)S(1)} %get-tuple-element.86), channel_id=1, source_target_pairs={{0,1},{1,2},{2,3},{3,4},{4,5},{5,6},{6,7},{7,8},{8,9},{9,10},{10,1... | collective-permute-start | bytes 786440 | tf_op jit(solution)/shard_map/ppermute | solution.py:23
  82.2 9.2 %collective-permute-start.5 = (f32[4,2,8192]{2,1,0:T(2,128)S(1)}, f32[4,2,8192]{2,1,0:T(2,128)S(1)}, u32[]{:S(2)}, u32[]{:S(2)}) collective-permute-start(f32[4,2,8192]{2,1,0:T(2,128)S(1)} %get-tuple-element.87), channel_id=1, source_target_pairs={{1,0},{2,1},{3,2},{4,3},{5,4},{6,5},{7,6},{8,7},{9,8},{10,9},{11,1... | collective-permute-start | bytes 786440 | tf_op jit(solution)/shard_map/ppermute | solution.py:25
  93.9 1.4 copy-start.5
  105.2 1.4 copy-start.6
  105.2 1.4 copy-start.16
  105.3 1.6 copy-start.17
  110.2 9.7 %collective-permute-start.6 = (f32[3,2,8192]{2,1,0:T(2,128)S(1)}, f32[3,2,8192]{2,1,0:T(2,128)S(1)}, u32[]{:S(2)}, u32[]{:S(2)}) collective-permute-start(f32[3,2,8192]{2,1,0:T(2,128)S(1)} %get-tuple-element.85), channel_id=1, source_target_pairs={{1,0},{2,1},{3,2},{4,3},{5,4},{6,5},{7,6},{8,7},{9,8},{10,9},{11,1... | collective-permute-start | bytes 589832 | tf_op jit(solution)/shard_map/ppermute | solution.py:12
  116.8 10.1 %copy-start.4 = (f32[1,2,8,8192]{3,2,1,0:T(8,128)S(1)}, f32[1,2,8,8192]{3,2,1,0:T(8,128)}, u32[]{:S(2)}) copy-start(f32[1,2,8,8192]{3,2,1,0:T(8,128)} %copy-done.2) | copy-start | bytes 1572868
  116.9 9.8 %collective-permute-start.7 = (f32[3,2,8192]{2,1,0:T(2,128)S(1)}, f32[3,2,8192]{2,1,0:T(2,128)S(1)}, u32[]{:S(2)}, u32[]{:S(2)}) collective-permute-start(f32[3,2,8192]{2,1,0:T(2,128)S(1)} %get-tuple-element.84), channel_id=1, source_target_pairs={{0,1},{1,2},{2,3},{3,4},{4,5},{5,6},{6,7},{7,8},{8,9},{9,10},{10,1... | collective-permute-start | bytes 589832 | tf_op jit(solution)/shard_map/ppermute | solution.py:12
  120.1 7.0 %copy-start.1 = (f32[4,12,8192]{2,1,0:T(8,128)S(1)}, f32[4,12,8192]{2,1,0:T(8,128)}, u32[]{:S(2)}) copy-start(f32[4,12,8192]{2,1,0:T(8,128)} %copy-done) | copy-start | bytes 4718596
  120.1 7.0 %copy-start.8 = (f32[10,8192]{1,0:T(8,128)S(1)}, f32[10,8192]{1,0:T(8,128)}, u32[]{:S(2)}) copy-start(f32[10,8192]{1,0:T(8,128)} %copy-done.7) | copy-start | bytes 983044
  120.1 7.0 %copy-start.14 = (f32[10,8192]{1,0:T(8,128)S(1)}, f32[10,8192]{1,0:T(8,128)}, u32[]{:S(2)}) copy-start(f32[10,8192]{1,0:T(8,128)} %get-tuple-element.75) | copy-start | bytes 983044
  120.1 7.0 %copy-start.15 = (f32[10,8192]{1,0:T(8,128)S(1)}, f32[10,8192]{1,0:T(8,128)}, u32[]{:S(2)}) copy-start(f32[10,8192]{1,0:T(8,128)} %get-tuple-element.109) | copy-start | bytes 983044
  128.9 6.2 %collective-permute-start.8 = (f32[1,2,8192]{2,1,0:T(2,128)S(1)}, f32[1,2,8192]{2,1,0:T(2,128)S(1)}, u32[]{:S(2)}, u32[]{:S(2)}) collective-permute-start(f32[1,2,8192]{2,1,0:T(2,128)S(1)} %get-tuple-element.93), channel_id=1, source_target_pairs={{1,0},{2,1},{3,2},{4,3},{5,4},{6,5},{7,6},{8,7},{9,8},{10,9},{11,1... | collective-permute-start | bytes 196616 | tf_op jit(solution)/shard_map/ppermute | solution.py:12
  130.8 8.3 %collective-permute-start.9 = (f32[1,2,8192]{2,1,0:T(2,128)S(1)}, f32[1,2,8192]{2,1,0:T(2,128)S(1)}, u32[]{:S(2)}, u32[]{:S(2)}) collective-permute-start(f32[1,2,8192]{2,1,0:T(2,128)S(1)} %get-tuple-element.92), channel_id=1, source_target_pairs={{0,1},{1,2},{2,3},{3,4},{4,5},{5,6},{6,7},{7,8},{8,9},{9,10},{10,1... | collective-permute-start | bytes 196616 | tf_op jit(solution)/shard_map/ppermute | solution.py:12
  (4 other events, 3.2 us)
Sparse Core Ops, SparseCore 0:
  140.0 69.2 all-reduce.29
where the time goes:
time: 218 us
  waiting for transfers between devices  98 us (45%)
  starting transfers between devices  61.7 us (28%)
  other arithmetic  28.1 us (13%)
  local copies, waits for them, and re-layouts  15.7 us (7%)
  between operations  14.1 us (6%)
    psum x1, waiting for transfers between devices, per_device(): total = lax.psum(local_grad, 'event')  69.4 us
    ppermute x3, starting transfers between devices, padded_2(): lax.ppermute(head, axis, [((i + 1) % count, i) for i in range(ends)])  19.6 us
    ppermute x4, starting transfers between devices, shifted(): lax.ppermute(value, axis, [(source, source + steps) for source in range(i...  14.4 us
    all_to_all x1, starting transfers between devices, per_device(): lax.all_to_all(send_cells.reshape(tile_count, capacity), 'tile', split_ax...  12.4 us
    ppermute x4, waiting for transfers between devices, shifted(): lax.ppermute(value, axis, [(source, source + steps) for source in range(i...  11.8 us
    all_to_all x1, waiting for transfers between devices, per_device(): lax.all_to_all(send_cells.reshape(tile_count, capacity), 'tile', split_ax...  10.1 us
    ppermute x3, starting transfers between devices, padded_2(): lax.ppermute(tail, axis, [(i, (i + 1) % count) for i in range(ends)])  9.78 us
    all_to_all x1, starting transfers between devices, per_device(): lax.all_to_all(send_values.reshape(tile_count, capacity), 'tile', split_a...  5.45 us
  transfers between devices with their start and end apart: 13, of which 9 were waited for; matrix products, arithmetic and copies ran while one was open for 6% of the time, Pallas kernels for 0%

commit v1 on v0

--- a/solution.py
+++ b/solution.py
@@ -155,7 +155,9 @@
             folded = fold_rims(jnp.stack((back_surface, back_east, back_north)), 2)
             sense_surface, sense_east, sense_north = (folded[0], folded[1], folded[2])
     local_grad = fold_rims(rough_sense[None], width)[0]
-    total = lax.psum(local_grad, "event")
+    total = local_grad
+    for hop in (1, 2, 4):
+        total = total + lax.ppermute(total, "event", [(dev, dev ^ hop) for dev in range(8)])
     share = col_count // lax.axis_size("event")
     return lax.dynamic_slice_in_dim(total, lax.axis_index("event") * share, share, 1)
 

time: 218 us -> 159 us (0.73)
  the two profiles are of different devices: /device:TPU:2 before, /device:TPU:18 now
where the time goes in v1:
time: 159 us; the launch traced here: 158 us
  starting transfers between devices  69 us (43%)
  waiting for transfers between devices  45.8 us (29%)
  other arithmetic  28.8 us (18%)
  local copies, waits for them, and re-layouts  13.6 us (9%)
    ppermute x3, starting transfers between devices, padded_2(): lax.ppermute(head, axis, [((i + 1) % count, i) for i in range(ends)])  19.7 us
    ppermute x3, waiting for transfers between devices, per_device(): lax.ppermute(total, 'event', [(dev, dev ^ hop) for dev in range(8)])  17.2 us
    ppermute x4, starting transfers between devices, shifted(): lax.ppermute(value, axis, [(source, source + steps) for source in range(i...  14.4 us
    all_to_all x1, starting transfers between devices, per_device(): lax.all_to_all(send_cells.reshape(tile_count, capacity), 'tile', split_ax...  12.4 us
    ppermute x4, waiting for transfers between devices, shifted(): lax.ppermute(value, axis, [(source, source + steps) for source in range(i...  11.8 us
    all_to_all x1, waiting for transfers between devices, per_device(): lax.all_to_all(send_cells.reshape(tile_count, capacity), 'tile', split_ax...  10.1 us
    ppermute x3, starting transfers between devices, padded_2(): lax.ppermute(tail, axis, [(i, (i + 1) % count) for i in range(ends)])  9.69 us
    ppermute x3, starting transfers between devices, per_device(): lax.ppermute(total, 'event', [(dev, dev ^ hop) for dev in range(8)])  7.36 us
  transfers between devices with their start and end apart: 15, of which 11 were waited for; matrix products, arithmetic and copies ran while one was open for 8% of the time, Pallas kernels for 0%

profile of v1, /device:TPU:18, one launch (start us, length us, event | category | flops | bytes accessed | tf_op | source)
XLA Modules:
  0.0 158.0 jit_solution(10710406579113047772)
XLA Ops:
  1.4 3.8 %collective-permute-start = (f32[2,2,8192]{2,1,0:T(2,128)S(1)}, f32[2,2,8192]{2,1,0:T(2,128)S(1)}, u32[]{:S(2)}, u32[]{:S(2)}) collective-permute-start(f32[2,2,8192]{2,1,0:T(2,128)S(1)} %get-tuple-element.102), channel_id=1, source_target_pairs={{0,1},{1,2},{2,3},{3,4},{4,5},{5,6},{6,7},{7,8},{8,9},{9,10},{10,1... | collective-permute-start | bytes 393224 | tf_op jit(solution)/shard_map/ppermute | solution.py:23
  5.2 9.5 %collective-permute-start.1 = (f32[2,2,8192]{2,1,0:T(2,128)S(1)}, f32[2,2,8192]{2,1,0:T(2,128)}, u32[]{:S(2)}, u32[]{:S(2)}) collective-permute-start(f32[2,2,8192]{2,1,0:T(2,128)S(1)} %get-tuple-element.103), channel_id=1, source_target_pairs={{1,0},{2,1},{3,2},{4,3},{5,4},{6,5},{7,6},{8,7},{9,8},{10,9},{11,1... | collective-permute-start | bytes 393224 | tf_op jit(solution)/shard_map/ppermute | solution.py:25
  17.7 1.6 scatter_custom_fusion
  19.9 12.4 %all-to-all-start = ((s32[64,1,8]{2,1,0:T(1,128)}), s32[64,1,8]{2,1,0:T(1,128)S(1)}, u32[]{:S(2)}, u32[]{:S(2)}) async-start(s32[64,1,8]{2,1,0:T(1,128)} %bitcast.12), calls=%async_computation | async-start | bytes 65536 | tf_op jit(solution)/shard_map/all_to_all | solution.py:114
  33.5 1.6 scatter_custom_fusion.1
  35.7 10.1 %all-to-all-done = s32[64,1,8]{2,1,0:T(1,128)S(1)} async-done(((s32[64,1,8]{2,1,0:T(1,128)}), s32[64,1,8]{2,1,0:T(1,128)S(1)}, u32[]{:S(2)}, u32[]{:S(2)}) %all-to-all-start) | async-done | bytes 2080 | tf_op jit(solution)/shard_map/all_to_all | solution.py:114
  45.8 5.5 %all-to-all-start.1 = ((f32[64,1,8]{2,1,0:T(1,128)}), f32[64,1,8]{2,1,0:T(1,128)S(1)}, u32[]{:S(2)}, u32[]{:S(2)}) async-start(f32[64,1,8]{2,1,0:T(1,128)} %bitcast.32), calls=%async_computation.1 | async-start | bytes 65536 | tf_op jit(solution)/shard_map/all_to_all | solution.py:121
  52.3 3.4 %collective-permute-start.2 = (f32[4,2,8192]{2,1,0:T(2,128)}, f32[4,2,8192]{2,1,0:T(2,128)S(1)}, u32[]{:S(2)}, u32[]{:S(2)}) collective-permute-start(f32[4,2,8192]{2,1,0:T(2,128)} %get-tuple-element.88), channel_id=1, source_target_pairs={{0,1},{1,2},{2,3},{3,4},{4,5},{5,6},{6,7},{7,8},{8,9},{9,10},{10,1... | collective-permute-start | bytes 786440 | tf_op jit(solution)/shard_map/ppermute | solution.py:23
  55.7 4.6 %collective-permute-start.3 = (f32[4,2,8192]{2,1,0:T(2,128)}, f32[4,2,8192]{2,1,0:T(2,128)S(1)}, u32[]{:S(2)}, u32[]{:S(2)}) collective-permute-start(f32[4,2,8192]{2,1,0:T(2,128)} %get-tuple-element.89), channel_id=1, source_target_pairs={{1,0},{2,1},{3,2},{4,3},{5,4},{6,5},{7,6},{8,7},{9,8},{10,9},{11,1... | collective-permute-start | bytes 786440 | tf_op jit(solution)/shard_map/ppermute | solution.py:25
  61.8 3.1 %all-to-all-done.1 = f32[64,1,8]{2,1,0:T(1,128)S(1)} async-done(((f32[64,1,8]{2,1,0:T(1,128)}), f32[64,1,8]{2,1,0:T(1,128)S(1)}, u32[]{:S(2)}, u32[]{:S(2)}) %all-to-all-start.1) | async-done | bytes 2080 | tf_op jit(solution)/shard_map/all_to_all | solution.py:121
  69.4 2.0 %fusion.58 = (f32[10,8192]{1,0:T(8,128)S(1)}, f32[10,8192]{1,0:T(8,128)S(1)}, f32[10,8192]{1,0:T(8,128)}) fusion(f32[2,12,8192]{2,1,0:T(8,128)S(1)} %pad_maximum_fusion.3, f32[4,12,8192]{2,1,0:T(8,128)S(1)} %pad_maximum_fusion, f32[10,8192]{1,0:T(8,128)S(1)} %slice_bitcast_fusion.5), kind=kLoop, calls=%fused_computation.162 | loop fusion | flops 1392640 | bytes 2949120 | tf_op jit(solution)/shard_map/div | solution.py:54
  73.2 2.5 %collective-permute-start.4 = (f32[4,2,8192]{2,1,0:T(2,128)S(1)}, f32[4,2,8192]{2,1,0:T(2,128)S(1)}, u32[]{:S(2)}, u32[]{:S(2)}) collective-permute-start(f32[4,2,8192]{2,1,0:T(2,128)S(1)} %get-tuple-element.86), channel_id=1, source_target_pairs={{0,1},{1,2},{2,3},{3,4},{4,5},{5,6},{6,7},{7,8},{8,9},{9,10},{10,1... | collective-permute-start | bytes 786440 | tf_op jit(solution)/shard_map/ppermute | solution.py:23
  75.7 5.6 %collective-permute-start.5 = (f32[4,2,8192]{2,1,0:T(2,128)S(1)}, f32[4,2,8192]{2,1,0:T(2,128)S(1)}, u32[]{:S(2)}, u32[]{:S(2)}) collective-permute-start(f32[4,2,8192]{2,1,0:T(2,128)S(1)} %get-tuple-element.87), channel_id=1, source_target_pairs={{1,0},{2,1},{3,2},{4,3},{5,4},{6,5},{7,6},{8,7},{9,8},{10,9},{11,1... | collective-permute-start | bytes 786440 | tf_op jit(solution)/shard_map/ppermute | solution.py:25
  81.4 2.2 %collective-permute-done.4 = f32[4,2,8192]{2,1,0:T(2,128)S(1)} collective-permute-done((f32[4,2,8192]{2,1,0:T(2,128)S(1)}, f32[4,2,8192]{2,1,0:T(2,128)S(1)}, u32[]{:S(2)}, u32[]{:S(2)}) %collective-permute-start.4) | collective-permute-done | bytes 262176 | tf_op jit(solution)/shard_map/ppermute | solution.py:23
  83.6 1.5 collective-permute-done.5
  85.4 2.0 %fusion.55 = (f32[10,8192]{1,0:T(8,128)S(1)}, f32[10,8192]{1,0:T(8,128)}, f32[10,8192]{1,0:T(8,128)S(1)}) fusion(f32[10,8192]{1,0:T(8,128)S(1)} %slice_bitcast_fusion.1, f32[2,12,8192]{2,1,0:T(8,128)S(1)} %pad_maximum_fusion.3, f32[4,12,8192]{2,1,0:T(8,128)S(1)} %pad_maximum_fusion.1), kind=kLoop, calls=%fused_computation.160 | loop fusion | flops 1392640 | bytes 2949120 | tf_op jit(solution)/shard_map/div | solution.py:54
  90.7 3.1 %gather_fusion = f32[512]{0:T(512)S(1)} fusion(f32[65536]{0:T(1024)S(1)} %bitcast.247, s32[1024]{0:T(1024)S(1)} %pad_clamp_fusion), kind=kCustom, calls=%fused_computation | custom fusion | bytes 6144 | tf_op jit(solution)/shard_map/jit(_take)/gather | solution.py:131
  93.9 3.9 %scatter_custom_fusion.2 = f32[65536]{0:T(1024)} fusion(s32[512]{0:T(512)S(1)} %bitcast.260, f32[512]{0:T(512)S(1)} %subtract_select_fusion, f32[]{:T(128)} %constant.144.clone.1), kind=kCustom, calls=%fused_computation.127 | custom fusion | flops 512 | bytes 262148 | tf_op jit(solution)/shard_map/scatter-add | solution.py:136
  100.4 1.7 %fusion = (f32[10,8192]{1,0:T(8,128)S(1)}, f32[10,8192]{1,0:T(8,128)S(1)}, f32[10,8192]{1,0:T(8,128)S(1)}, f32[10,8192]{1,0:T(8,128)S(1)}, f32[10,8192]{1,0:T(8,128)S(1)}) fusion(f32[2,12,8192]{2,1,0:T(8,128)S(1)} %pad_maximum_fusion.3, f32[4,12,8192]{2,1,0:T(8,128)S(1)} %pad_maximum_fusion.1, f32[10,8192]{1,0:T(8,128)S(1)} %copy-done.16, ...), kind=kLoop, calls=%fused_computation.14 | loop fusion | flops 2621440 | bytes 5439528 | tf_op jit(solution)/shard_map/transpose(jvp())/add_any | solution.py:52
  103.8 6.5 %collective-permute-start.6 = (f32[3,2,8192]{2,1,0:T(2,128)S(1)}, f32[3,2,8192]{2,1,0:T(2,128)S(1)}, u32[]{:S(2)}, u32[]{:S(2)}) collective-permute-start(f32[3,2,8192]{2,1,0:T(2,128)S(1)} %get-tuple-element.85), channel_id=1, source_target_pairs={{1,0},{2,1},{3,2},{4,3},{5,4},{6,5},{7,6},{8,7},{9,8},{10,9},{11,1... | collective-permute-start | bytes 589832 | tf_op jit(solution)/shard_map/ppermute | solution.py:12
  110.5 2.1 %collective-permute-start.7 = (f32[3,2,8192]{2,1,0:T(2,128)S(1)}, f32[3,2,8192]{2,1,0:T(2,128)S(1)}, u32[]{:S(2)}, u32[]{:S(2)}) collective-permute-start(f32[3,2,8192]{2,1,0:T(2,128)S(1)} %get-tuple-element.84), channel_id=1, source_target_pairs={{0,1},{1,2},{2,3},{3,4},{4,5},{5,6},{6,7},{7,8},{8,9},{9,10},{10,1... | collective-permute-start | bytes 589832 | tf_op jit(solution)/shard_map/ppermute | solution.py:12
  113.7 6.6 %collective-permute-done.7 = f32[3,2,8192]{2,1,0:T(2,128)S(1)} collective-permute-done((f32[3,2,8192]{2,1,0:T(2,128)S(1)}, f32[3,2,8192]{2,1,0:T(2,128)S(1)}, u32[]{:S(2)}, u32[]{:S(2)}) %collective-permute-start.7) | collective-permute-done | bytes 196640 | tf_op jit(solution)/shard_map/ppermute | solution.py:12
  120.7 1.5 fusion.1
  122.4 1.9 %collective-permute-start.8 = (f32[1,2,8192]{2,1,0:T(2,128)S(1)}, f32[1,2,8192]{2,1,0:T(2,128)S(1)}, u32[]{:S(2)}, u32[]{:S(2)}) collective-permute-start(f32[1,2,8192]{2,1,0:T(2,128)S(1)} %get-tuple-element.93), channel_id=1, source_target_pairs={{1,0},{2,1},{3,2},{4,3},{5,4},{6,5},{7,6},{8,7},{9,8},{10,9},{11,1... | collective-permute-start | bytes 196616 | tf_op jit(solution)/shard_map/ppermute | solution.py:12
  124.4 3.9 %collective-permute-start.9 = (f32[1,2,8192]{2,1,0:T(2,128)S(1)}, f32[1,2,8192]{2,1,0:T(2,128)S(1)}, u32[]{:S(2)}, u32[]{:S(2)}) collective-permute-start(f32[1,2,8192]{2,1,0:T(2,128)S(1)} %get-tuple-element.92), channel_id=1, source_target_pairs={{0,1},{1,2},{2,3},{3,4},{4,5},{5,6},{6,7},{7,8},{8,9},{9,10},{10,1... | collective-permute-start | bytes 196616 | tf_op jit(solution)/shard_map/ppermute | solution.py:12
  128.7 4.0 %collective-permute-done.9 = f32[1,2,8192]{2,1,0:T(2,128)S(1)} collective-permute-done((f32[1,2,8192]{2,1,0:T(2,128)S(1)}, f32[1,2,8192]{2,1,0:T(2,128)S(1)}, u32[]{:S(2)}, u32[]{:S(2)}) %collective-permute-start.9) | collective-permute-done | bytes 65568 | tf_op jit(solution)/shard_map/ppermute | solution.py:12
  132.7 1.9 %collective-permute-start.10 = (f32[8,8192]{1,0:T(8,128)S(1)}, f32[8,8192]{1,0:T(8,128)S(1)}, u32[]{:S(2)}, u32[]{:S(2)}) collective-permute-start(f32[8,8192]{1,0:T(8,128)S(1)} %fusion.42), channel_id=1, source_target_pairs={{0,64},{64,0},{128,192},{192,128},{256,320},{320,256},{384,448},{4... | collective-permute-start | bytes 786440 | tf_op jit(solution)/shard_map/ppermute | solution.py:160
  134.7 1.5 collective-permute-done.10
  136.2 3.2 %collective-permute-start.11 = (f32[8,8192]{1,0:T(8,128)S(1)}, f32[8,8192]{1,0:T(8,128)S(1)}, u32[]{:S(2)}, u32[]{:S(2)}) collective-permute-start(f32[8,8192]{1,0:T(8,128)S(1)} %add.191), channel_id=1, source_target_pairs={{0,128},{64,192},{128,0},{192,64},{256,384},{320,448},{384,256},{4... | collective-permute-start | bytes 786440 | tf_op jit(solution)/shard_map/ppermute | solution.py:160
  139.4 7.0 %collective-permute-done.11 = f32[8,8192]{1,0:T(8,128)S(1)} collective-permute-done((f32[8,8192]{1,0:T(8,128)S(1)}, f32[8,8192]{1,0:T(8,128)S(1)}, u32[]{:S(2)}, u32[]{:S(2)}) %collective-permute-start.11) | collective-permute-done | bytes 262176 | tf_op jit(solution)/shard_map/ppermute | solution.py:160
  146.5 2.2 %collective-permute-start.12 = (f32[8,8192]{1,0:T(8,128)S(1)}, f32[8,8192]{1,0:T(8,128)S(1)}, u32[]{:S(2)}, u32[]{:S(2)}) collective-permute-start(f32[8,8192]{1,0:T(8,128)S(1)} %add.192), channel_id=1, source_target_pairs={{0,256},{64,320},{128,384},{192,448},{256,0},{320,64},{384,128},{4... | collective-permute-start | bytes 786440 | tf_op jit(solution)/shard_map/ppermute | solution.py:160
  148.7 8.6 %collective-permute-done.12 = f32[8,8192]{1,0:T(8,128)S(1)} collective-permute-done((f32[8,8192]{1,0:T(8,128)S(1)}, f32[8,8192]{1,0:T(8,128)S(1)}, u32[]{:S(2)}, u32[]{:S(2)}) %collective-permute-start.12) | collective-permute-done | bytes 262176 | tf_op jit(solution)/shard_map/ppermute | solution.py:160
  (114 shorter events, 26.2 us)
Async XLA Ops:
  0.0 51.3 %copy-start.9 = (f32[1,8,8192]{2,1,0:T(8,128)S(1)}, f32[1,8,8192]{2,1,0:T(8,128)}, u32[]{:S(2)}) copy-start(f32[1,8,8192]{2,1,0:T(8,128)} %param.18) | copy-start | bytes 786436
  0.0 51.3 %copy-start.12 = (f32[1,8,8192]{2,1,0:T(8,128)S(1)}, f32[1,8,8192]{2,1,0:T(8,128)}, u32[]{:S(2)}) copy-start(f32[1,8,8192]{2,1,0:T(8,128)} %param.19) | copy-start | bytes 786436
  0.0 51.3 %copy-start.10 = (f32[1,8,8192]{2,1,0:T(8,128)S(1)}, f32[1,8,8192]{2,1,0:T(8,128)}, u32[]{:S(2)}) copy-start(f32[1,8,8192]{2,1,0:T(8,128)} %param.20) | copy-start | bytes 786436
  1.4 64.9 %collective-permute-start = (f32[2,2,8192]{2,1,0:T(2,128)S(1)}, f32[2,2,8192]{2,1,0:T(2,128)S(1)}, u32[]{:S(2)}, u32[]{:S(2)}) collective-permute-start(f32[2,2,8192]{2,1,0:T(2,128)S(1)} %get-tuple-element.102), channel_id=1, source_target_pairs={{0,1},{1,2},{2,3},{3,4},{4,5},{5,6},{6,7},{7,8},{8,9},{9,10},{10,1... | collective-permute-start | bytes 393224 | tf_op jit(solution)/shard_map/ppermute | solution.py:23
  5.2 61.1 %collective-permute-start.1 = (f32[2,2,8192]{2,1,0:T(2,128)S(1)}, f32[2,2,8192]{2,1,0:T(2,128)}, u32[]{:S(2)}, u32[]{:S(2)}) collective-permute-start(f32[2,2,8192]{2,1,0:T(2,128)S(1)} %get-tuple-element.103), channel_id=1, source_target_pairs={{1,0},{2,1},{3,2},{4,3},{5,4},{6,5},{7,6},{8,7},{9,8},{10,9},{11,1... | collective-permute-start | bytes 393224 | tf_op jit(solution)/shard_map/ppermute | solution.py:25
  19.9 25.9 %all-to-all-start = ((s32[64,1,8]{2,1,0:T(1,128)}), s32[64,1,8]{2,1,0:T(1,128)S(1)}, u32[]{:S(2)}, u32[]{:S(2)}) async-start(s32[64,1,8]{2,1,0:T(1,128)} %bitcast.12), calls=%async_computation | async-start | bytes 65536 | tf_op jit(solution)/shard_map/all_to_all | solution.py:114
  33.4 39.4 %copy-start.2 = (f32[1,2,8,8192]{3,2,1,0:T(8,128)}, f32[1,2,8,8192]{3,2,1,0:T(8,128)S(1)}, u32[]{:S(2)}) copy-start(f32[1,2,8,8192]{3,2,1,0:T(8,128)S(1)} %convert_element_type.19) | copy-start | bytes 1572868
  45.8 19.1 %all-to-all-start.1 = ((f32[64,1,8]{2,1,0:T(1,128)}), f32[64,1,8]{2,1,0:T(1,128)S(1)}, u32[]{:S(2)}, u32[]{:S(2)}) async-start(f32[64,1,8]{2,1,0:T(1,128)} %bitcast.32), calls=%async_computation.1 | async-start | bytes 65536 | tf_op jit(solution)/shard_map/all_to_all | solution.py:121
  52.3 15.2 %collective-permute-start.2 = (f32[4,2,8192]{2,1,0:T(2,128)}, f32[4,2,8192]{2,1,0:T(2,128)S(1)}, u32[]{:S(2)}, u32[]{:S(2)}) collective-permute-start(f32[4,2,8192]{2,1,0:T(2,128)} %get-tuple-element.88), channel_id=1, source_target_pairs={{0,1},{1,2},{2,3},{3,4},{4,5},{5,6},{6,7},{7,8},{8,9},{9,10},{10,1... | collective-permute-start | bytes 786440 | tf_op jit(solution)/shard_map/ppermute | solution.py:23
  55.7 11.9 %collective-permute-start.3 = (f32[4,2,8192]{2,1,0:T(2,128)}, f32[4,2,8192]{2,1,0:T(2,128)S(1)}, u32[]{:S(2)}, u32[]{:S(2)}) collective-permute-start(f32[4,2,8192]{2,1,0:T(2,128)} %get-tuple-element.89), channel_id=1, source_target_pairs={{1,0},{2,1},{3,2},{4,3},{5,4},{6,5},{7,6},{8,7},{9,8},{10,9},{11,1... | collective-permute-start | bytes 786440 | tf_op jit(solution)/shard_map/ppermute | solution.py:25
  69.3 2.1 %copy-start = (f32[4,12,8192]{2,1,0:T(8,128)}, f32[4,12,8192]{2,1,0:T(8,128)S(1)}, u32[]{:S(2)}) copy-start(f32[4,12,8192]{2,1,0:T(8,128)S(1)} %pad_maximum_fusion) | copy-start | bytes 4718596
  69.4 2.1 %copy-start.11 = (f32[1,8,8192]{2,1,0:T(8,128)S(1)}, f32[1,8,8192]{2,1,0:T(8,128)}, u32[]{:S(2)}) copy-start(f32[1,8,8192]{2,1,0:T(8,128)} %param.20) | copy-start | bytes 786436
  69.4 2.1 %copy-start.13 = (f32[1,8,8192]{2,1,0:T(8,128)S(1)}, f32[1,8,8192]{2,1,0:T(8,128)}, u32[]{:S(2)}) copy-start(f32[1,8,8192]{2,1,0:T(8,128)} %param.19) | copy-start | bytes 786436
  69.4 2.1 %copy-start.19 = (f32[4,2,8192]{2,1,0:T(2,128)S(1)}, f32[4,2,8192]{2,1,0:T(2,128)}, u32[]{:S(2)}) copy-start(f32[4,2,8192]{2,1,0:T(2,128)} %copy-done.18) | copy-start | bytes 786436
  69.4 2.1 %copy-start.21 = (f32[4,2,8192]{2,1,0:T(2,128)S(1)}, f32[4,2,8192]{2,1,0:T(2,128)}, u32[]{:S(2)}) copy-start(f32[4,2,8192]{2,1,0:T(2,128)} %copy-done.20) | copy-start | bytes 786436
  71.4 1.5 copy-start.7
  73.2 10.4 %collective-permute-start.4 = (f32[4,2,8192]{2,1,0:T(2,128)S(1)}, f32[4,2,8192]{2,1,0:T(2,128)S(1)}, u32[]{:S(2)}, u32[]{:S(2)}) collective-permute-start(f32[4,2,8192]{2,1,0:T(2,128)S(1)} %get-tuple-element.86), channel_id=1, source_target_pairs={{0,1},{1,2},{2,3},{3,4},{4,5},{5,6},{6,7},{7,8},{8,9},{9,10},{10,1... | collective-permute-start | bytes 786440 | tf_op jit(solution)/shard_map/ppermute | solution.py:23
  75.7 9.3 %collective-permute-start.5 = (f32[4,2,8192]{2,1,0:T(2,128)S(1)}, f32[4,2,8192]{2,1,0:T(2,128)S(1)}, u32[]{:S(2)}, u32[]{:S(2)}) collective-permute-start(f32[4,2,8192]{2,1,0:T(2,128)S(1)} %get-tuple-element.87), channel_id=1, source_target_pairs={{1,0},{2,1},{3,2},{4,3},{5,4},{6,5},{7,6},{8,7},{9,8},{10,9},{11,1... | collective-permute-start | bytes 786440 | tf_op jit(solution)/shard_map/ppermute | solution.py:25
  87.4 1.5 copy-start.5
  98.8 1.6 copy-start.17
  103.8 9.7 %collective-permute-start.6 = (f32[3,2,8192]{2,1,0:T(2,128)S(1)}, f32[3,2,8192]{2,1,0:T(2,128)S(1)}, u32[]{:S(2)}, u32[]{:S(2)}) collective-permute-start(f32[3,2,8192]{2,1,0:T(2,128)S(1)} %get-tuple-element.85), channel_id=1, source_target_pairs={{1,0},{2,1},{3,2},{4,3},{5,4},{6,5},{7,6},{8,7},{9,8},{10,9},{11,1... | collective-permute-start | bytes 589832 | tf_op jit(solution)/shard_map/ppermute | solution.py:12
  110.4 10.1 %copy-start.4 = (f32[1,2,8,8192]{3,2,1,0:T(8,128)S(1)}, f32[1,2,8,8192]{3,2,1,0:T(8,128)}, u32[]{:S(2)}) copy-start(f32[1,2,8,8192]{3,2,1,0:T(8,128)} %copy-done.2) | copy-start | bytes 1572868
  110.5 9.8 %collective-permute-start.7 = (f32[3,2,8192]{2,1,0:T(2,128)S(1)}, f32[3,2,8192]{2,1,0:T(2,128)S(1)}, u32[]{:S(2)}, u32[]{:S(2)}) collective-permute-start(f32[3,2,8192]{2,1,0:T(2,128)S(1)} %get-tuple-element.84), channel_id=1, source_target_pairs={{0,1},{1,2},{2,3},{3,4},{4,5},{5,6},{6,7},{7,8},{8,9},{9,10},{10,1... | collective-permute-start | bytes 589832 | tf_op jit(solution)/shard_map/ppermute | solution.py:12
  113.7 7.0 %copy-start.1 = (f32[4,12,8192]{2,1,0:T(8,128)S(1)}, f32[4,12,8192]{2,1,0:T(8,128)}, u32[]{:S(2)}) copy-start(f32[4,12,8192]{2,1,0:T(8,128)} %copy-done) | copy-start | bytes 4718596
  113.7 7.0 %copy-start.8 = (f32[10,8192]{1,0:T(8,128)S(1)}, f32[10,8192]{1,0:T(8,128)}, u32[]{:S(2)}) copy-start(f32[10,8192]{1,0:T(8,128)} %copy-done.7) | copy-start | bytes 983044
  113.7 7.0 %copy-start.14 = (f32[10,8192]{1,0:T(8,128)S(1)}, f32[10,8192]{1,0:T(8,128)}, u32[]{:S(2)}) copy-start(f32[10,8192]{1,0:T(8,128)} %get-tuple-element.75) | copy-start | bytes 983044
  113.7 7.0 %copy-start.15 = (f32[10,8192]{1,0:T(8,128)S(1)}, f32[10,8192]{1,0:T(8,128)}, u32[]{:S(2)}) copy-start(f32[10,8192]{1,0:T(8,128)} %get-tuple-element.109) | copy-start | bytes 983044
  122.4 6.2 %collective-permute-start.8 = (f32[1,2,8192]{2,1,0:T(2,128)S(1)}, f32[1,2,8192]{2,1,0:T(2,128)S(1)}, u32[]{:S(2)}, u32[]{:S(2)}) collective-permute-start(f32[1,2,8192]{2,1,0:T(2,128)S(1)} %get-tuple-element.93), channel_id=1, source_target_pairs={{1,0},{2,1},{3,2},{4,3},{5,4},{6,5},{7,6},{8,7},{9,8},{10,9},{11,1... | collective-permute-start | bytes 196616 | tf_op jit(solution)/shard_map/ppermute | solution.py:12
  124.4 8.3 %collective-permute-start.9 = (f32[1,2,8192]{2,1,0:T(2,128)S(1)}, f32[1,2,8192]{2,1,0:T(2,128)S(1)}, u32[]{:S(2)}, u32[]{:S(2)}) collective-permute-start(f32[1,2,8192]{2,1,0:T(2,128)S(1)} %get-tuple-element.92), channel_id=1, source_target_pairs={{0,1},{1,2},{2,3},{3,4},{4,5},{5,6},{6,7},{7,8},{8,9},{9,10},{10,1... | collective-permute-start | bytes 196616 | tf_op jit(solution)/shard_map/ppermute | solution.py:12
  132.7 3.4 %collective-permute-start.10 = (f32[8,8192]{1,0:T(8,128)S(1)}, f32[8,8192]{1,0:T(8,128)S(1)}, u32[]{:S(2)}, u32[]{:S(2)}) collective-permute-start(f32[8,8192]{1,0:T(8,128)S(1)} %fusion.42), channel_id=1, source_target_pairs={{0,64},{64,0},{128,192},{192,128},{256,320},{320,256},{384,448},{4... | collective-permute-start | bytes 786440 | tf_op jit(solution)/shard_map/ppermute | solution.py:160
  136.2 10.2 %collective-permute-start.11 = (f32[8,8192]{1,0:T(8,128)S(1)}, f32[8,8192]{1,0:T(8,128)S(1)}, u32[]{:S(2)}, u32[]{:S(2)}) collective-permute-start(f32[8,8192]{1,0:T(8,128)S(1)} %add.191), channel_id=1, source_target_pairs={{0,128},{64,192},{128,0},{192,64},{256,384},{320,448},{384,256},{4... | collective-permute-start | bytes 786440 | tf_op jit(solution)/shard_map/ppermute | solution.py:160
  146.5 10.9 %collective-permute-start.12 = (f32[8,8192]{1,0:T(8,128)S(1)}, f32[8,8192]{1,0:T(8,128)S(1)}, u32[]{:S(2)}, u32[]{:S(2)}) collective-permute-start(f32[8,8192]{1,0:T(8,128)S(1)} %add.192), channel_id=1, source_target_pairs={{0,256},{64,320},{128,384},{192,448},{256,0},{320,64},{384,128},{4... | collective-permute-start | bytes 786440 | tf_op jit(solution)/shard_map/ppermute | solution.py:160
  (5 other events, 5.3 us)
